TPU v7x, 32 devices: a whole 2x2x4 slice. The times are simulated.
32 devices in a mesh: pipe: 16 (over z, y, core), tensor: 2 (over x).
Axes of the slice: x: 2, y: 2, z: 4, core: 2. Of those that a mesh axis runs over, the one named last changes fastest.
Arguments:
- up_weight: bfloat16 [16, 6400, 3200], P('pipe', 'tensor'), may hold values from -0.109375 to 0.109375
- down_weight: bfloat16 [16, 6400, 3200], P('pipe', 'tensor'), may hold values from -0.078125 to 0.078125
- norm_gain: float32 [16, 3200], P('pipe'), may hold values from 0.1 to 1.9
- layer_scale: float32 [16, 3200], P('pipe'), may hold values from 0.25 to 1
- stash: bfloat16 [16, 3, 256, 3200], P('pipe', None, 'tensor'), may hold values from -6 to 6
- slot_order: int32 [16, 3], P('pipe'), may hold values from 0 to 2, each once within a row
- received: float32 [16, 256, 3200], P('pipe', 'tensor'), may hold values from -6 to 6
- arrivals: bfloat16 [3, 64, 12800], P(None, 'tensor'), may hold values from -6 to 6
Outputs:
- emitted: bfloat16 [16, 3, 256, 3200], P('pipe', None, 'tensor')
- pending: float32 [16, 256, 3200], P('pipe', 'tensor')
Inputs may be any that keep to these rules, and one draw needn't show every extreme that they name: `slot_order`: each section's row is an ordering of the slots 0 to 2.
All inputs are finite; a program needn't handle non-finite values.
Results may differ from a plain program's by a relative error of at most 0.02.
Values may be sent and summed in bfloat16 or wider, within the bound.
A program may use at most 128 MiB of HBM per device.

v0:
```python
import jax
import jax.numpy as jnp
from jax import lax
from jax.sharding import PartitionSpec as P

GRID = 16


EPS = 1e-06


def passed_along(block, axis, distance):
    devices = range(lax.axis_size(axis))
    route = [(i - distance, i) for i in devices if i - distance in devices]
    return lax.ppermute(block, axis, route)


def gelu_slope(hidden):
    return (
        0.5 * (1.0 + jax.scipy.special.erf(hidden * 0.7071067811865476))
        + hidden * jnp.exp(-0.5 * hidden * hidden) * 0.3989422804014327
    )


def norm_parts(stash_rows):
    values = stash_rows.astype(jnp.float32)
    factor = lax.rsqrt(jnp.mean(values * values, axis=-1, keepdims=True) + EPS)
    return (factor, values * factor)


def recompute(stash_rows, gain, up_w, down_w, scaled):
    factor, normed = norm_parts(stash_rows)
    act = (normed * gain).astype(jnp.bfloat16)
    dims = (((1,), (1,)), ((), ()))
    hidden = lax.dot_general(act, up_w, dims, preferred_element_type=jnp.float32)
    upstream = lax.dot_general(scaled, down_w, dims, preferred_element_type=jnp.float32)
    return (upstream * gelu_slope(hidden)).astype(jnp.bfloat16)


def norm_back(stash_rows, gain, total):
    factor, normed = norm_parts(stash_rows)
    scaled_back = total * gain
    return factor * (scaled_back - normed * jnp.mean(scaled_back * normed, axis=-1, keepdims=True))


def shards(up_weight, down_weight, norm_gain, layer_scale, stash, slot_order, received, arrivals):
    up_w = up_weight[0]
    down_w = down_weight[0]
    gain = norm_gain[0]
    lscale = layer_scale[0]
    rows = received.shape[1]
    width = received.shape[2]
    ticks = stash.shape[1]
    half = GRID // 2
    lines = rows // 4 // half
    landed = (
        arrivals.reshape(ticks, lines, half, 2, 2, width)
        .transpose(0, 1, 3, 2, 4, 5)
        .reshape(ticks, rows, width)
    )
    is_last = lax.axis_index("pipe") == lax.axis_size("pipe") - 1
    outputs = []
    grads = received[0]
    for tick in range(ticks):
        stash_rows = lax.dynamic_index_in_dim(stash[0], slot_order[0, tick], 0, keepdims=False)
        scaled = (grads * lscale).astype(jnp.bfloat16)
        full_stash, full_scaled = (
            lax.all_gather(stash_rows, "tensor", axis=0, tiled=True),
            lax.all_gather(scaled, "tensor", axis=0, tiled=True),
        )
        slope = recompute(full_stash, gain, up_w, down_w, full_scaled)
        total = lax.psum_scatter(
            jnp.dot(slope, up_w, preferred_element_type=jnp.float32).astype(jnp.bfloat16),
            "tensor",
            scatter_dimension=0,
            tiled=True,
        ).astype(jnp.float32)
        moved = grads + norm_back(stash_rows, gain, total)
        outputs.append(moved.astype(jnp.bfloat16))
        incoming = passed_along(moved.astype(jnp.bfloat16), "pipe", -1).astype(moved.dtype)
        grads = jnp.where(is_last, landed[tick].astype(jnp.float32), incoming)
    return (jnp.stack(outputs, axis=0)[None], grads[None])


def solution(mesh):
    return jax.shard_map(
        shards,
        mesh=mesh,
        in_specs=(
            P("pipe", "tensor", None),
            P("pipe", "tensor", None),
            P("pipe", None),
            P("pipe", None),
            P("pipe", None, "tensor", None),
            P("pipe", None),
            P("pipe", "tensor", None),
            P(None, "tensor", None),
        ),
        out_specs=(P("pipe", None, "tensor", None), P("pipe", "tensor", None)),
        check_vma=False,
    )
```

profile of v0, /device:TPU:1, one launch (start us, length us, event | category | flops | bytes accessed | tf_op | source)
XLA Modules:
  0.0 374.2 jit_solution(11581541926394065805)
XLA Ops:
  14.1 4.0 %fusion.110 = (f32[128]{0:T(128)}, bf16[1,1,128,3200]{3,2,1,0:T(8,128)(2,1)}, f32[128]{0:T(128)S(1)}, bf16[1,1,128,3200]{3,2,1,0:T(8,128)(2,1)}, f32[128]{0:T(128)S(1)}, /*index=5*/bf16[1,1,128,3200]{3,2,1,0:T(8,128)(2,1)}) fusion(bf16[1,3,128,3200]{3,2,1,0:T(8,128)(2,1)} %param.12, s32[]{:T(128)S(6)} %select_n.31, s32[]{:T(128)S(6)} %select_n.26, ...), kind=kLoop, calls=%fused_computation.100 | loop fusion | flops 3686016 | bytes 4916748 | tf_op jit(solution)/shard_map/reduce_sum | solution.py:27
  19.4 28.7 %all-gather.16.cloned.1.call-done = bf16[1,1,256,3200]{3,2,1,0:T(8,128)(2,1)} async-done(((bf16[1,1,128,3200]{3,2,1,0:T(8,128)(2,1)}), bf16[1,1,256,3200]{3,2,1,0:T(8,128)(2,1)}) %all-gather.16.cloned.1.call-update) | async-done | bytes 1638416 | tf_op jit(solution)/shard_map/all_gather | solution.py:68
  50.1 12.5 %fusion.10 = f32[256,3200]{1,0:T(8,128)} fusion(bf16[1,3200,3200]{2,1,0:T(8,128)(2,1)} %param.8, bf16[1,1,256,3200]{3,2,1,0:T(8,128)(2,1)S(1)} %copy-done.10, f32[3200]{0:T(1024)S(1)} %reduce.1, f32[256]{0:T(256)S(1)} %add_rsqrt_fusion.2), kind=kOutput, calls=%fused_computation.10 | convolution fusion | flops 5246156800 | bytes 25409024 | tf_op jit(solution)/shard_map/dot_general | solution.py:35
  62.6 15.6 %all-gather.10.cloned.1.call-done = bf16[256,3200]{1,0:T(8,128)(2,1)} async-done(((bf16[128,3200]{1,0:T(8,128)(2,1)}), bf16[256,3200]{1,0:T(8,128)(2,1)}) %all-gather.10.cloned.1.call-update) | async-done | bytes 1638416 | tf_op jit(solution)/shard_map/all_gather | solution.py:69
  78.2 22.8 %fusion.27 = bf16[256,3200]{1,0:T(8,128)(2,1)} fusion(bf16[1,3200,3200]{2,1,0:T(8,128)(2,1)} %param.8, bf16[256,3200]{1,0:T(8,128)(2,1)} %all-gather.10.cloned.1.call-done, bf16[1,3200,3200]{2,1,0:T(8,128)(2,1)} %param.9, f32[256,3200]{1,0:T(8,128)} %fusion.10), kind=kOutput, calls=%fused_computation.21 | convolution fusion | flops 10494771200 | bytes 47513600 | tf_op jit(solution)/shard_map/dot_general | solution.py:73
  101.7 3.7 copy.12
  105.4 22.7 %reduce-scatter.4.cloned.1.call-done = bf16[128,3200]{1,0:T(8,128)(2,1)} async-done(((bf16[256,3200]{1,0:T(8,128)(2,1)}), bf16[128,3200]{1,0:T(8,128)(2,1)}) %reduce-scatter.4.cloned.1.call-update) | async-done | bytes 819216 | tf_op jit(solution)/shard_map/reduce_scatter | solution.py:72
  129.8 2.6 fusion.107
  132.5 2.9 collective-permute-start
  135.4 2.9 slice_convert_fusion
  140.8 16.6 %all-gather.18.cloned.1.call-done = bf16[1,1,256,3200]{3,2,1,0:T(8,128)(2,1)} async-done(((bf16[1,1,128,3200]{3,2,1,0:T(8,128)(2,1)}), bf16[1,1,256,3200]{3,2,1,0:T(8,128)(2,1)}) %all-gather.18.cloned.1.call-update) | async-done | bytes 1638416 | tf_op jit(solution)/shard_map/all_gather | solution.py:68
  160.6 12.2 %fusion.6 = f32[256,3200]{1,0:T(8,128)} fusion(bf16[1,3200,3200]{2,1,0:T(8,128)(2,1)} %param.8, bf16[1,1,256,3200]{3,2,1,0:T(8,128)(2,1)} %all-gather.18.cloned.1.call-done, f32[256]{0:T(256)S(1)} %add_rsqrt_fusion.1, f32[3200]{0:T(1024)S(1)} %reduce.1), kind=kOutput, calls=%fused_computation.6 | convolution fusion | flops 5246156800 | bytes 25409024 | tf_op jit(solution)/shard_map/dot_general | solution.py:35
  172.9 15.8 %all-gather.12.cloned.1.call-done = bf16[256,3200]{1,0:T(8,128)(2,1)} async-done(((bf16[128,3200]{1,0:T(8,128)(2,1)}), bf16[256,3200]{1,0:T(8,128)(2,1)}) %all-gather.12.cloned.1.call-update) | async-done | bytes 1638416 | tf_op jit(solution)/shard_map/all_gather | solution.py:69
  188.6 22.8 %fusion.30 = bf16[256,3200]{1,0:T(8,128)(2,1)} fusion(bf16[1,3200,3200]{2,1,0:T(8,128)(2,1)} %param.8, bf16[256,3200]{1,0:T(8,128)(2,1)} %all-gather.12.cloned.1.call-done, bf16[1,3200,3200]{2,1,0:T(8,128)(2,1)} %param.9, f32[256,3200]{1,0:T(8,128)} %fusion.6), kind=kOutput, calls=%fused_computation.22 | convolution fusion | flops 10494771200 | bytes 47513600 | tf_op jit(solution)/shard_map/dot_general | solution.py:73
  212.3 26.2 %reduce-scatter.6.cloned.1.call-done = bf16[128,3200]{1,0:T(8,128)(2,1)} async-done(((bf16[256,3200]{1,0:T(8,128)(2,1)}), bf16[128,3200]{1,0:T(8,128)(2,1)}) %reduce-scatter.6.cloned.1.call-update) | async-done | bytes 819216 | tf_op jit(solution)/shard_map/reduce_scatter | solution.py:72
  242.0 3.0 collective-permute-start.1
  247.4 20.6 %all-gather.20.cloned.1.call-done = bf16[1,1,256,3200]{3,2,1,0:T(8,128)(2,1)} async-done(((bf16[1,1,128,3200]{3,2,1,0:T(8,128)(2,1)}), bf16[1,1,256,3200]{3,2,1,0:T(8,128)(2,1)}) %all-gather.20.cloned.1.call-update) | async-done | bytes 1638416 | tf_op jit(solution)/shard_map/all_gather | solution.py:68
  271.1 12.2 %fusion.2 = f32[256,3200]{1,0:T(8,128)} fusion(bf16[1,3200,3200]{2,1,0:T(8,128)(2,1)} %param.8, bf16[1,1,256,3200]{3,2,1,0:T(8,128)(2,1)} %all-gather.20.cloned.1.call-done, f32[256]{0:T(256)S(1)} %add_rsqrt_fusion, f32[3200]{0:T(1024)S(1)} %reduce.1), kind=kOutput, calls=%fused_computation.2 | convolution fusion | flops 5246156800 | bytes 25409024 | tf_op jit(solution)/shard_map/dot_general | solution.py:35
  283.4 15.8 %all-gather.14.cloned.1.call-done = bf16[256,3200]{1,0:T(8,128)(2,1)} async-done(((bf16[128,3200]{1,0:T(8,128)(2,1)}), bf16[256,3200]{1,0:T(8,128)(2,1)}) %all-gather.14.cloned.1.call-update) | async-done | bytes 1638416 | tf_op jit(solution)/shard_map/all_gather | solution.py:69
  299.1 22.8 %fusion.33 = bf16[256,3200]{1,0:T(8,128)(2,1)} fusion(bf16[1,3200,3200]{2,1,0:T(8,128)(2,1)} %param.8, bf16[256,3200]{1,0:T(8,128)(2,1)} %all-gather.14.cloned.1.call-done, bf16[1,3200,3200]{2,1,0:T(8,128)(2,1)} %param.9, f32[256,3200]{1,0:T(8,128)} %fusion.2), kind=kOutput, calls=%fused_computation.23 | convolution fusion | flops 10494771200 | bytes 47513600 | tf_op jit(solution)/shard_map/dot_general | solution.py:73
  322.6 26.4 %reduce-scatter.8.cloned.1.call-done = bf16[128,3200]{1,0:T(8,128)(2,1)} async-done(((bf16[256,3200]{1,0:T(8,128)(2,1)}), bf16[128,3200]{1,0:T(8,128)(2,1)}) %reduce-scatter.8.cloned.1.call-update) | async-done | bytes 819216 | tf_op jit(solution)/shard_map/reduce_scatter | solution.py:72
  352.3 2.7 collective-permute-start.2
  357.5 3.1 maximum_bitcast_fusion
  360.6 5.7 %collective-permute-done.2 = bf16[128,3200]{1,0:T(8,128)(2,1)S(1)} collective-permute-done((bf16[128,3200]{1,0:T(8,128)(2,1)}, bf16[128,3200]{1,0:T(8,128)(2,1)S(1)}, u32[]{:S(2)}, u32[]{:S(2)}) %collective-permute-start.2) | collective-permute-done | bytes 819232 | tf_op jit(solution)/shard_map/ppermute | solution.py:15
  (75 shorter events, 30.0 us)
Async XLA Ops:
  7.2 41.0 %all-gather.16.cloned.1.call-start = ((), (), s32[]{:S(2)}) async-start(), calls=%async_computation.9 | async-start | bytes 2457600 | tf_op jit(solution)/shard_map/all_gather | solution.py:68
  14.1 4.1 %copy-start.11 = (f32[1,3200]{1,0:T(1,128)S(1)}, f32[1,3200]{1,0:T(1,128)}, u32[]{:S(2)}) copy-start(f32[1,3200]{1,0:T(1,128)} %param.11) | copy-start | bytes 38404
  14.1 4.1 %copy-start.3 = (f32[1,128,3200]{2,1,0:T(8,128)S(1)}, f32[1,128,3200]{2,1,0:T(8,128)}, u32[]{:S(2)}) copy-start(f32[1,128,3200]{2,1,0:T(8,128)} %param.14) | copy-start | bytes 4915204
  18.2 60.0 %all-gather.10.cloned.1.call-start = ((), (), s32[]{:S(2)}) async-start(), calls=%async_computation.3 | async-start | bytes 2457600 | tf_op jit(solution)/shard_map/all_gather | solution.py:69
  19.3 108.8 %reduce-scatter.4.cloned.1.call-start = ((), (), s32[]{:S(2)}) async-start(), calls=%async_computation.4 | async-start | bytes 2457600 | tf_op jit(solution)/shard_map/reduce_scatter | solution.py:72
  48.1 2.0 copy-start.10
  101.0 56.4 %all-gather.18.cloned.1.call-start = ((), (), s32[]{:S(2)}) async-start(), calls=%async_computation.10 | async-start | bytes 2457600 | tf_op jit(solution)/shard_map/all_gather | solution.py:68
  101.6 87.0 %all-gather.12.cloned.1.call-start = ((), (), s32[]{:S(2)}) async-start(), calls=%async_computation.5 | async-start | bytes 2457600 | tf_op jit(solution)/shard_map/all_gather | solution.py:69
  101.7 26.4 %copy-start.2 = (bf16[1,1,128,3200]{3,2,1,0:T(8,128)(2,1)S(1)}, bf16[1,1,128,3200]{3,2,1,0:T(8,128)(2,1)}, u32[]{:S(2)}) copy-start(bf16[1,1,128,3200]{3,2,1,0:T(8,128)(2,1)} %get-tuple-element.12) | copy-start | bytes 2457604
  128.1 1.7 copy-start.4
  132.5 26.8 %collective-permute-start = (bf16[128,3200]{1,0:T(8,128)(2,1)}, bf16[128,3200]{1,0:T(8,128)(2,1)S(1)}, u32[]{:S(2)}, u32[]{:S(2)}) collective-permute-start(bf16[128,3200]{1,0:T(8,128)(2,1)} %fusion.107), channel_id=1, source_target_pairs={{2,0},{4,2},{6,4},{8,6},{10,8},{12,10},{14,12},{16,14},{18,16},{20... | collective-permute-start | bytes 2457608 | tf_op jit(solution)/shard_map/ppermute | solution.py:15
  159.3 1.2 copy-start.5
  160.6 78.0 %reduce-scatter.6.cloned.1.call-start = ((), (), s32[]{:S(2)}) async-start(), calls=%async_computation.6 | async-start | bytes 2457600 | tf_op jit(solution)/shard_map/reduce_scatter | solution.py:72
  211.5 27.1 %copy-start.1 = (bf16[1,1,128,3200]{3,2,1,0:T(8,128)(2,1)S(1)}, bf16[1,1,128,3200]{3,2,1,0:T(8,128)(2,1)}, u32[]{:S(2)}) copy-start(bf16[1,1,128,3200]{3,2,1,0:T(8,128)(2,1)} %get-tuple-element.14) | copy-start | bytes 2457604
  211.5 56.5 %all-gather.20.cloned.1.call-start = ((), (), s32[]{:S(2)}) async-start(), calls=%async_computation.11 | async-start | bytes 2457600 | tf_op jit(solution)/shard_map/all_gather | solution.py:68
  212.2 86.9 %all-gather.14.cloned.1.call-start = ((), (), s32[]{:S(2)}) async-start(), calls=%async_computation.7 | async-start | bytes 2457600 | tf_op jit(solution)/shard_map/all_gather | solution.py:69
  238.5 1.7 copy-start.8
  242.0 27.9 %collective-permute-start.1 = (bf16[128,3200]{1,0:T(8,128)(2,1)S(1)}, bf16[128,3200]{1,0:T(8,128)(2,1)S(1)}, u32[]{:S(2)}, u32[]{:S(2)}) collective-permute-start(bf16[128,3200]{1,0:T(8,128)(2,1)S(1)} %fusion.102), channel_id=1, source_target_pairs={{2,0},{4,2},{6,4},{8,6},{10,8},{12,10},{14,12},{16,14},{18,16},{20... | collective-permute-start | bytes 2457608 | tf_op jit(solution)/shard_map/ppermute | solution.py:15
  269.9 1.2 copy-start.6
  271.1 78.0 %reduce-scatter.8.cloned.1.call-start = ((), (), s32[]{:S(2)}) async-start(), calls=%async_computation.8 | async-start | bytes 2457600 | tf_op jit(solution)/shard_map/reduce_scatter | solution.py:72
  322.0 27.1 %copy-start = (bf16[1,1,128,3200]{3,2,1,0:T(8,128)(2,1)S(1)}, bf16[1,1,128,3200]{3,2,1,0:T(8,128)(2,1)}, u32[]{:S(2)}) copy-start(bf16[1,1,128,3200]{3,2,1,0:T(8,128)(2,1)} %get-tuple-element.3) | copy-start | bytes 2457604
  349.0 1.7 copy-start.7
  349.0 1.7 copy-start.9
  352.3 14.0 %collective-permute-start.2 = (bf16[128,3200]{1,0:T(8,128)(2,1)}, bf16[128,3200]{1,0:T(8,128)(2,1)S(1)}, u32[]{:S(2)}, u32[]{:S(2)}) collective-permute-start(bf16[128,3200]{1,0:T(8,128)(2,1)} %fusion.97), channel_id=1, source_target_pairs={{2,0},{4,2},{6,4},{8,6},{10,8},{12,10},{14,12},{16,14},{18,16},{20... | collective-permute-start | bytes 2457608 | tf_op jit(solution)/shard_map/ppermute | solution.py:15
  (2 other events, 1.7 us)
Sparse Core Ops, SparseCore 0:
  18.3 29.8 all-gather.15
  50.2 27.9 all-gather.9
  101.2 26.8 reduce-scatter.3
  129.5 27.9 all-gather.17
  160.7 27.8 all-gather.11
  211.6 26.8 reduce-scatter.5
  240.1 27.9 all-gather.19
  271.2 27.9 all-gather.13
  322.1 26.8 reduce-scatter.7
where the time goes:
time: 375 us; the launch traced here: 374 us
  waiting for transfers between devices  196 us (52%)
  matrix products  105 us (28%)
  other arithmetic  31.5 us (8%)
  between operations  19.6 us (5%)
  local copies, waits for them, and re-layouts  13.1 us (3%)
  starting transfers between devices  8.99 us (2%)
    reduce_scatter x3, waiting for transfers between devices, shards(): lax.psum_scatter(jnp.dot(slope, up_w, preferred_element_type=jnp.float32)...  75.4 us
    dot_general x3, matrix products, shards(): jnp.dot(slope, up_w, preferred_element_type=jnp.float32)  68.5 us
    all_gather x3, waiting for transfers between devices, shards(): lax.all_gather(stash_rows, 'tensor', axis=0, tiled=True)  65.9 us
    all_gather x3, waiting for transfers between devices, shards(): lax.all_gather(scaled, 'tensor', axis=0, tiled=True)  47.2 us
    dot_general x3, matrix products, recompute(): lax.dot_general(act, up_w, dims, preferred_element_type=jnp.float32)  37 us
    reduce_sum x4, other arithmetic, norm_parts(): factor = lax.rsqrt(jnp.mean(values * values, axis=-1, keepdims=True) + EPS)  9.61 us
    ppermute x3, starting transfers between devices, passed_along(): return lax.ppermute(block, axis, route)  8.62 us
  transfers between devices with their start and end apart: 12, of which 10 were waited for; matrix products, arithmetic and copies ran while one was open for 18% of the time, Pallas kernels for 0%

commit v1 on v0

v1 whole, which is shorter than its diff:
```python
import functools

import jax
import jax.numpy as jnp
from jax import lax
from jax.experimental import pallas as pl
from jax.experimental.pallas import tpu as pltpu
from jax.sharding import PartitionSpec as P

GRID = 16
EPS = 1e-06
CHUNKS = 4
RING = 4
TILE = 512
MESH = pl.DeviceIdType.MESH
NT = (((1,), (1,)), ((), ()))


def gelu_slope(hidden):
    return (
        0.5 * (1.0 + lax.erf(hidden * 0.7071067811865476))
        + hidden * jnp.exp(-0.5 * hidden * hidden) * 0.3989422804014327
    )


def tiles_of(size):
    return size // TILE, size % TILE


def kernel(
    n, sections, steps, order, gain, lscale, up_hbm, down_hbm, stash_hbm, received_hbm, landed_hbm,
    out_hbm, pend_hbm,
    up_w, down_w, stash, grads, landed, act, scaled, slope, psend, precv, gin, moved_b,
    wsem, isem, a_send, a_recv, s_send, s_recv, p_send, p_recv, g_send, g_recv, o_sem, e_sem,
):
    hid, width = up_w.shape
    rows = grads.shape[1]
    me = lax.axis_index("tensor")
    sec = lax.axis_index("pipe")
    has_next = sec > 0
    has_prev = sec < sections - 1
    is_last = sec == sections - 1
    full, rem = tiles_of(hid)
    wfull, wrem = tiles_of(width)

    def peer(d):
        return lax.rem(me + d, n)

    in_stash = pltpu.make_async_copy(stash_hbm, stash, isem.at[0])
    in_grads = pltpu.make_async_copy(received_hbm, grads, isem.at[1])
    in_landed = pltpu.make_async_copy(landed_hbm, landed, isem.at[2])
    in_stash.start()
    in_grads.start()

    def weight_copies(j, size):
        first = j * TILE
        if not isinstance(j, int):
            first = pl.multiple_of(first, TILE)
        span = pl.ds(first, size)
        return (
            pltpu.make_async_copy(up_hbm.at[span], up_w.at[span], wsem.at[0, j]),
            pltpu.make_async_copy(down_hbm.at[span], down_w.at[span], wsem.at[1, j]),
        )

    for j in range(full + (rem > 0)):
        for copy in weight_copies(j, TILE if j < full else rem):
            copy.start()
    in_landed.start()

    barrier = pltpu.get_barrier_semaphore()
    for d in range(1, n):
        pl.semaphore_signal(barrier, inc=1, device_id={"tensor": peer(d)}, device_id_type=MESH)

    @pl.when(has_next)
    def _():
        pl.semaphore_signal(barrier, inc=1, device_id={"pipe": sec - 1}, device_id_type=MESH)

    @pl.when(has_prev)
    def _():
        pl.semaphore_signal(barrier, inc=1, device_id={"pipe": sec + 1}, device_id_type=MESH)

    def stash_rows(q):
        tick, chunk = q // CHUNKS, q % CHUNKS
        values = stash[order[0, tick], chunk].astype(jnp.float32)
        factor = lax.rsqrt(jnp.mean(values * values, axis=-1, keepdims=True) + EPS)
        return factor, values * factor

    def spread(buf, send, recv, slot, d):
        return pltpu.make_async_remote_copy(
            src_ref=buf.at[slot, me],
            dst_ref=buf.at[slot, me],
            send_sem=send.at[slot, d - 1],
            recv_sem=recv.at[slot, d - 1],
            device_id={"tensor": peer(d)},
            device_id_type=MESH,
        )

    def part_copy(slot, d):
        return pltpu.make_async_remote_copy(
            src_ref=psend.at[slot, peer(d)],
            dst_ref=precv.at[slot, d - 1],
            send_sem=p_send.at[slot, d - 1],
            recv_sem=p_recv.at[slot, d - 1],
            device_id={"tensor": peer(d)},
            device_id_type=MESH,
        )

    def pipe_copy(q):
        return pltpu.make_async_remote_copy(
            src_ref=moved_b.at[q],
            dst_ref=gin.at[q],
            send_sem=g_send.at[q],
            recv_sem=g_recv.at[q],
            device_id={"pipe": jnp.maximum(sec - 1, 0)},
            device_id_type=MESH,
        )

    def out_copy(q):
        return pltpu.make_async_copy(moved_b.at[q], out_hbm.at[q], o_sem.at[q])

    def send_act(q):
        slot = q % RING
        _, normed = stash_rows(q)
        act[slot, me] = (normed * gain[...]).astype(jnp.bfloat16)
        for d in range(1, n):
            spread(act, a_send, a_recv, slot, d).start()

    def send_scaled(q):
        slot = q % RING
        scaled[slot, me] = (grads[q % CHUNKS] * lscale[...]).astype(jnp.bfloat16)
        for d in range(1, n):
            spread(scaled, s_send, s_recv, slot, d).start()

    def finish(q):
        slot, chunk = q % RING, q % CHUNKS
        for d in range(1, n):
            part_copy(slot, d).wait_recv()
        total = psend[slot, me].astype(jnp.float32)
        for d in range(1, n):
            total += precv[slot, d - 1].astype(jnp.float32)
        factor, normed = stash_rows(q)
        back = total * gain[...]
        moved = grads[chunk] + factor * (back - normed * jnp.mean(back * normed, axis=-1, keepdims=True))
        moved_b[q] = moved.astype(jnp.bfloat16)

        @pl.when(has_next)
        def _():
            pipe_copy(q).start()

        out_copy(q).start()

    def next_grads(q):
        chunk, before = q % CHUNKS, q - CHUNKS

        @pl.when(is_last)
        def _():
            grads[chunk] = landed[before].astype(jnp.float32)

        @pl.when(has_prev)
        def _():
            pipe_copy(before).wait_recv()
            grads[chunk] = gin[before].astype(jnp.float32)

    in_stash.wait()
    in_grads.wait()
    heads = min(2, steps)
    for q in range(heads):
        slot = q % RING
        _, normed = stash_rows(q)
        act[slot, me] = (normed * gain[...]).astype(jnp.bfloat16)
        scaled[slot, me] = (grads[q % CHUNKS] * lscale[...]).astype(jnp.bfloat16)
        if q == 0:
            waits = (n - 1) + has_next.astype(jnp.int32) + has_prev.astype(jnp.int32)
            pl.semaphore_wait(barrier, waits)
        for d in range(1, n):
            spread(act, a_send, a_recv, slot, d).start()
        for d in range(1, n):
            spread(scaled, s_send, s_recv, slot, d).start()
    in_landed.wait()

    tokens = n * rows

    def step(q, carry):
        slot = q % RING
        for d in range(1, n):
            spread(act, a_send, a_recv, slot, d).wait_recv()
            spread(scaled, s_send, s_recv, slot, d).wait_recv()

        def up_tile(j, size):
            @pl.when(q == 0)
            def _():
                for copy in weight_copies(j, size):
                    copy.wait()

            first = j * TILE
            if not isinstance(j, int):
                first = pl.multiple_of(first, TILE)
            span = pl.ds(first, size)
            hidden = lax.dot_general(
                act[slot].reshape(tokens, width), up_w[span, :], NT, preferred_element_type=jnp.float32
            )
            upstream = lax.dot_general(
                scaled[slot].reshape(tokens, width), down_w[span, :], NT, preferred_element_type=jnp.float32
            )
            slope[:, span] = (upstream * gelu_slope(hidden)).astype(jnp.bfloat16)

        pl.loop(0, full)(lambda j: up_tile(j, TILE))
        if rem:
            up_tile(full, rem)

        @pl.when(q >= RING)
        def _():
            for d in range(1, n):
                part_copy(slot, d).wait_send()

        def down_tile(j, size):
            first = j * TILE
            if not isinstance(j, int):
                first = pl.multiple_of(first, TILE)
            span = pl.ds(first, size)
            part = jnp.dot(slope[...], up_w[:, span], preferred_element_type=jnp.float32)
            psend[slot, :, :, span] = part.astype(jnp.bfloat16).reshape(n, rows, size)

        pl.loop(0, wfull)(lambda j: down_tile(j, TILE))
        if wrem:
            down_tile(wfull, wrem)
        for d in range(1, n):
            part_copy(slot, d).start()

        @pl.when(q >= 1)
        def _():
            finish(q - 1)

        @pl.when(q + heads < steps)
        def _():
            later = q + heads

            @pl.when(later >= RING)
            def _():
                for d in range(1, n):
                    spread(act, a_send, a_recv, later % RING, d).wait_send()
                    spread(scaled, s_send, s_recv, later % RING, d).wait_send()

            @pl.when(later >= CHUNKS)
            def _():
                next_grads(later)

            send_scaled(later)
            send_act(later)

        return carry

    lax.fori_loop(0, steps, step, 0)
    finish(steps - 1)

    for q in range(steps - CHUNKS, steps):
        @pl.when(has_prev)
        def _(q=q):
            pipe_copy(q).wait_recv()
            pltpu.make_async_copy(gin.at[q], pend_hbm.at[q - steps + CHUNKS], e_sem.at[q - steps + CHUNKS]).start()

    for q in range(steps):
        out_copy(q).wait()

        @pl.when(has_next)
        def _(q=q):
            pipe_copy(q).wait_send()

    for slot in range(min(RING, steps)):
        for d in range(1, n):
            spread(act, a_send, a_recv, slot, d).wait_send()
            spread(scaled, s_send, s_recv, slot, d).wait_send()
            part_copy(slot, d).wait_send()
    for c in range(CHUNKS):
        @pl.when(has_prev)
        def _(c=c):
            pltpu.make_async_copy(gin.at[steps - CHUNKS + c], pend_hbm.at[c], e_sem.at[c]).wait()


def shards(n, sections, up_weight, down_weight, norm_gain, layer_scale, stash, slot_order, received, arrivals):
    up_w, down_w = up_weight[0], down_weight[0]
    hid, width = up_w.shape
    _, ticks, tokens, _ = stash.shape
    half = GRID // 2
    lines = tokens // 4 // half
    rows = tokens // CHUNKS
    steps = ticks * CHUNKS
    landed = (
        arrivals.reshape(ticks, lines, half, 2, 2, width)
        .transpose(0, 1, 3, 2, 4, 5)
        .reshape(ticks, tokens, width)
    )
    bf = jnp.bfloat16
    hold = pl.BlockSpec(memory_space=pltpu.VMEM)
    far = pl.BlockSpec(memory_space=pl.ANY)
    dma = pltpu.SemaphoreType.DMA
    tile_count = hid // TILE + (hid % TILE > 0)
    out, pend = pl.pallas_call(
        functools.partial(kernel, n, sections, steps),
        out_shape=(
            jax.ShapeDtypeStruct((steps, rows, width), bf),
            jax.ShapeDtypeStruct((CHUNKS, rows, width), bf),
        ),
        in_specs=[pl.BlockSpec(memory_space=pltpu.SMEM), hold, hold, far, far, far, far, far],
        out_specs=(far, far),
        scratch_shapes=[
            pltpu.VMEM((hid, width), bf),
            pltpu.VMEM((hid, width), bf),
            pltpu.VMEM((ticks, CHUNKS, rows, width), bf),
            pltpu.VMEM((CHUNKS, rows, width), jnp.float32),
            pltpu.VMEM((steps, rows, width), bf),
            pltpu.VMEM((RING, n, rows, width), bf),
            pltpu.VMEM((RING, n, rows, width), bf),
            pltpu.VMEM((n * rows, hid), bf),
            pltpu.VMEM((RING, n, rows, width), bf),
            pltpu.VMEM((RING, n - 1, rows, width), bf),
            pltpu.VMEM((steps, rows, width), bf),
            pltpu.VMEM((steps, rows, width), bf),
            dma((2, tile_count)),
            dma((3,)),
            dma((RING, n - 1)),
            dma((RING, n - 1)),
            dma((RING, n - 1)),
            dma((RING, n - 1)),
            dma((RING, n - 1)),
            dma((RING, n - 1)),
            dma((steps,)),
            dma((steps,)),
            dma((steps,)),
            dma((CHUNKS,)),
        ],
        compiler_params=pltpu.CompilerParams(
            collective_id=0, has_side_effects=True, vmem_limit_bytes=66 * 1024 * 1024 - 2 * 1024 * 1024
        ),
    )(
        slot_order,
        norm_gain,
        layer_scale,
        up_w,
        down_w,
        stash.reshape(ticks, CHUNKS, rows, width),
        received.reshape(CHUNKS, rows, width),
        landed.reshape(steps, rows, width),
    )
    is_last = lax.axis_index("pipe") == sections - 1
    pending = jnp.where(is_last, landed[ticks - 1], pend.reshape(tokens, width)).astype(jnp.float32)
    return out.reshape(1, ticks, tokens, width), pending[None]


def solution(mesh):
    return jax.shard_map(
        functools.partial(shards, mesh.shape["tensor"], mesh.shape["pipe"]),
        mesh=mesh,
        in_specs=(
            P("pipe", "tensor", None),
            P("pipe", "tensor", None),
            P("pipe", None),
            P("pipe", None),
            P("pipe", None, "tensor", None),
            P("pipe", None),
            P("pipe", "tensor", None),
            P(None, "tensor", None),
        ),
        out_specs=(P("pipe", None, "tensor", None), P("pipe", "tensor", None)),
        check_vma=False,
    )
```

time: 375 us -> 267 us (0.71)
  Pallas kernels: 0 us -> 255 us
  waiting for transfers between devices: 196 us -> 0 us
  matrix products: 105 us -> 0 us
  other arithmetic: 31.5 us -> 2.59 us
  between operations: 19.6 us -> 0.66 us
  starting transfers between devices: 8.99 us -> 0 us
  local copies, waits for them, and re-layouts: 13.1 us -> 9.18 us
    pallas_call x0 -> x1, Pallas kernels: none -> 255 us  [shards(): pl.pallas_call(functools.partial(kernel, n, sections, steps), out_shape=(...]
    all_gather x6 -> x0, waiting for transfers between devices: 113 us -> none  [the longest x3 65.9 us: shards(): lax.all_gather(stash_rows, 'tensor', axis=0, tiled=True)]
    dot_general x6 -> x0, matrix products: 105 us -> none  [the longest x3 68.5 us: shards(): jnp.dot(slope, up_w, preferred_element_type=jnp.float32)]
    reduce_scatter x3 -> x0, waiting for transfers between devices: 75.4 us -> none  [shards(): lax.psum_scatter(jnp.dot(slope, up_w, preferred_element_type=jnp.float32)...]
    reduce_sum x7 -> x0, other arithmetic: 14.7 us -> none  [the longest x4 9.61 us: norm_parts(): factor = lax.rsqrt(jnp.mean(values * values, axis=-1, keepdims=True) + EPS)]
    convert_element_type x7 -> x1, other arithmetic: 12.2 us -> 2.59 us  [shards(): jnp.where(is_last, landed[ticks - 1], pend.reshape(tokens, width))]
    ppermute x3 -> x0, starting transfers between devices: 8.62 us -> none  [passed_along(): return lax.ppermute(block, axis, route)]
    convert_element_type x3 -> x0, local copies, waits for them, and re-layouts: 7.4 us -> none  [shards(): grads = jnp.where(is_last, landed[tick].astype(jnp.float32), incoming)]
  transfers between devices with their start and end apart: 12 -> 0, of which waited for: 10 -> 0; matrix products, arithmetic and copies ran while one was open for 18% -> 0% of each run, Pallas kernels for 0% -> 0%
where the time goes in v1:
time: 267 us
  Pallas kernels  255 us (96%)
  local copies, waits for them, and re-layouts  9.18 us (3%)
    pallas_call x1, Pallas kernels, shards(): pl.pallas_call(functools.partial(kernel, n, sections, steps), out_shape=(...  255 us

profile of v1, /device:TPU:1, one launch (start us, length us, event | category | flops | bytes accessed | tf_op | source)
XLA Modules:
  0.0 267.2 jit_solution(8276228969827932886)
XLA Ops:
  0.6 3.6 %copy.12 = bf16[3,4,8,2,2,3200]{5,4,2,3,1,0:T(2,128)(2,1)S(1)} copy(bf16[3,4,8,2,2,3200]{5,2,4,3,1,0:T(8,128)(2,1)} %bitcast.18) | data formatting | bytes 4915200 | tf_op jit(solution)/shard_map/reshape | solution.py:289
  4.2 0.6 slice.5
  4.8 2.4 reshape_reshape.3.landed_hbm
  7.2 1.2 squeeze.11
  8.4 254.7 %shard_map.95 = (bf16[12,32,3200]{2,1,0:T(8,128)(2,1)}, bf16[4,32,3200]{2,1,0:T(8,128)(2,1)}) custom-call(s32[1,3]{1,0:T(1,128)} %order.1, f32[1,3200]{1,0:T(1,128)} %gain.1, f32[1,3200]{1,0:T(1,128)} %lscale.1, bf16[3200,3200]{1,0:T(8,128)(2,1)} %bitcast.14, bf16[3200,3200]{1,0:T(8,128)(2,1)} %bitcast.15, bf16[3,4,32,3200]{3,2,1,0:T(8,128)(2,1)} %bitcast.20, ...), custom_call_target="tpu_custom_call" | custom-call | tf_op jit(solution)/shard_map/pallas_call | solution.py:298
  263.1 0.0 copy-start
  263.1 2.6 fusion
  265.7 0.0 copy-done
  265.7 1.4 copy.14
Async XLA Ops:
  263.1 2.6 copy-start

commit v2 on v1

--- a/solution.py
+++ b/solution.py
@@ -9,8 +9,9 @@
 
 GRID = 16
 EPS = 1e-06
-CHUNKS = 4
-RING = 4
+CHUNKS = 2
+RING = 2
+HELD = 2 * CHUNKS
 TILE = 512
 MESH = pl.DeviceIdType.MESH
 NT = (((1,), (1,)), ((), ()))
@@ -30,7 +31,7 @@
 def kernel(
     n, sections, steps, order, gain, lscale, up_hbm, down_hbm, stash_hbm, received_hbm, landed_hbm,
     out_hbm, pend_hbm,
-    up_w, down_w, stash, grads, landed, act, scaled, slope, psend, precv, gin, moved_b,
+    up_w, down_w, stash, grads, landed, act, scaled, factor_of, slope, psend, precv, gin, moved_b,
     wsem, isem, a_send, a_recv, s_send, s_recv, p_send, p_recv, g_send, g_recv, o_sem, e_sem,
 ):
     hid, width = up_w.shape
@@ -62,9 +63,9 @@
             pltpu.make_async_copy(down_hbm.at[span], down_w.at[span], wsem.at[1, j]),
         )
 
-    for j in range(full + (rem > 0)):
-        for copy in weight_copies(j, TILE if j < full else rem):
-            copy.start()
+    for which in range(2):
+        for j in range(full + (rem > 0)):
+            weight_copies(j, TILE if j < full else rem)[which].start()
     in_landed.start()
 
     barrier = pltpu.get_barrier_semaphore()
@@ -95,10 +96,10 @@
             device_id_type=MESH,
         )
 
-    def part_copy(slot, d):
+    def part_copy(slot, d, span=slice(None)):
         return pltpu.make_async_remote_copy(
-            src_ref=psend.at[slot, peer(d)],
-            dst_ref=precv.at[slot, d - 1],
+            src_ref=psend.at[slot, peer(d), :, span],
+            dst_ref=precv.at[slot, d - 1, :, span],
             send_sem=p_send.at[slot, d - 1],
             recv_sem=p_recv.at[slot, d - 1],
             device_id={"tensor": peer(d)},
@@ -118,18 +119,18 @@
     def out_copy(q):
         return pltpu.make_async_copy(moved_b.at[q], out_hbm.at[q], o_sem.at[q])
 
-    def send_act(q):
-        slot = q % RING
-        _, normed = stash_rows(q)
-        act[slot, me] = (normed * gain[...]).astype(jnp.bfloat16)
-        for d in range(1, n):
-            spread(act, a_send, a_recv, slot, d).start()
-
-    def send_scaled(q):
-        slot = q % RING
-        scaled[slot, me] = (grads[q % CHUNKS] * lscale[...]).astype(jnp.bfloat16)
-        for d in range(1, n):
-            spread(scaled, s_send, s_recv, slot, d).start()
+    def act_copy(a, d):
+        return spread(act, a_send, a_recv, a % HELD, d)
+
+    def make_act(a):
+        _, normed = stash_rows(a)
+        act[a % HELD, me] = (normed * gain[...]).astype(jnp.bfloat16)
+
+    def make_scaled(q):
+        scaled[q % RING, me] = (grads[q % CHUNKS] * lscale[...]).astype(jnp.bfloat16)
+
+    def scaled_copy(q, d):
+        return spread(scaled, s_send, s_recv, q % RING, d)
 
     def finish(q):
         slot, chunk = q % RING, q % CHUNKS
@@ -163,90 +164,110 @@
 
     in_stash.wait()
     in_grads.wait()
-    heads = min(2, steps)
-    for q in range(heads):
-        slot = q % RING
-        _, normed = stash_rows(q)
-        act[slot, me] = (normed * gain[...]).astype(jnp.bfloat16)
-        scaled[slot, me] = (grads[q % CHUNKS] * lscale[...]).astype(jnp.bfloat16)
-        if q == 0:
+    for a in range(CHUNKS):
+        make_act(a)
+        if a == 0:
             waits = (n - 1) + has_next.astype(jnp.int32) + has_prev.astype(jnp.int32)
             pl.semaphore_wait(barrier, waits)
         for d in range(1, n):
-            spread(act, a_send, a_recv, slot, d).start()
-        for d in range(1, n):
-            spread(scaled, s_send, s_recv, slot, d).start()
+            act_copy(a, d).start()
+    for q in range(CHUNKS):
+        make_scaled(q)
+        for d in range(1, n):
+            scaled_copy(q, d).start()
+    ahead = min(CHUNKS + 1, steps)
+    for a in range(CHUNKS, ahead):
+        make_act(a)
+        for d in range(1, n):
+            act_copy(a, d).start()
     in_landed.wait()
 
     tokens = n * rows
 
+    def aligned(j):
+        first = j * TILE
+        return first if isinstance(j, int) else pl.multiple_of(first, TILE)
+
     def step(q, carry):
-        slot = q % RING
-        for d in range(1, n):
-            spread(act, a_send, a_recv, slot, d).wait_recv()
-            spread(scaled, s_send, s_recv, slot, d).wait_recv()
-
-        def up_tile(j, size):
+        slot, chunk = q % RING, q % CHUNKS
+
+        def arrive(which, j, size):
             @pl.when(q == 0)
             def _():
-                for copy in weight_copies(j, size):
-                    copy.wait()
-
-            first = j * TILE
-            if not isinstance(j, int):
-                first = pl.multiple_of(first, TILE)
-            span = pl.ds(first, size)
-            hidden = lax.dot_general(
-                act[slot].reshape(tokens, width), up_w[span, :], NT, preferred_element_type=jnp.float32
-            )
+                weight_copies(j, size)[which].wait()
+
+        def hidden_tile(j, size):
+            arrive(0, j, size)
+            span = pl.ds(aligned(j), size)
+            rows_of = act[pl.ds(q % HELD, CHUNKS)].reshape(CHUNKS * tokens, width)
+            hidden = lax.dot_general(rows_of, up_w[span, :], NT, preferred_element_type=jnp.float32)
+            factor_of[:, :, span] = gelu_slope(hidden).reshape(CHUNKS, tokens, size)
+
+        @pl.when(chunk == 0)
+        def _():
+            for c in range(CHUNKS):
+                for d in range(1, n):
+                    act_copy(q + c, d).wait_recv()
+            pl.loop(0, full)(lambda j: hidden_tile(j, TILE))
+            if rem:
+                hidden_tile(full, rem)
+
+        for d in range(1, n):
+            scaled_copy(q, d).wait_recv()
+
+        def up_tile(j, size):
+            arrive(1, j, size)
+            span = pl.ds(aligned(j), size)
             upstream = lax.dot_general(
                 scaled[slot].reshape(tokens, width), down_w[span, :], NT, preferred_element_type=jnp.float32
             )
-            slope[:, span] = (upstream * gelu_slope(hidden)).astype(jnp.bfloat16)
+            slope[:, span] = (upstream * factor_of[chunk, :, span]).astype(jnp.bfloat16)
 
         pl.loop(0, full)(lambda j: up_tile(j, TILE))
         if rem:
             up_tile(full, rem)
 
+        @pl.when(q >= 1)
+        def _():
+            finish(q - 1)
+
         @pl.when(q >= RING)
         def _():
             for d in range(1, n):
                 part_copy(slot, d).wait_send()
 
         def down_tile(j, size):
-            first = j * TILE
-            if not isinstance(j, int):
-                first = pl.multiple_of(first, TILE)
-            span = pl.ds(first, size)
+            span = pl.ds(aligned(j), size)
             part = jnp.dot(slope[...], up_w[:, span], preferred_element_type=jnp.float32)
             psend[slot, :, :, span] = part.astype(jnp.bfloat16).reshape(n, rows, size)
+            for d in range(1, n):
+                part_copy(slot, d, span).start()
 
         pl.loop(0, wfull)(lambda j: down_tile(j, TILE))
         if wrem:
             down_tile(wfull, wrem)
-        for d in range(1, n):
-            part_copy(slot, d).start()
-
-        @pl.when(q >= 1)
-        def _():
-            finish(q - 1)
-
-        @pl.when(q + heads < steps)
-        def _():
-            later = q + heads
-
-            @pl.when(later >= RING)
+
+        @pl.when((q + 1 >= CHUNKS) & (q + 1 < steps))
+        def _():
+            for d in range(1, n):
+                scaled_copy(q + 1, d).wait_send()
+            next_grads(q + 1)
+            make_scaled(q + 1)
+            for d in range(1, n):
+                scaled_copy(q + 1, d).start()
+
+        @pl.when(q + ahead < steps)
+        def _():
+            later = q + ahead
+
+            @pl.when(later >= HELD)
             def _():
                 for d in range(1, n):
-                    spread(act, a_send, a_recv, later % RING, d).wait_send()
-                    spread(scaled, s_send, s_recv, later % RING, d).wait_send()
-
-            @pl.when(later >= CHUNKS)
-            def _():
-                next_grads(later)
-
-            send_scaled(later)
-            send_act(later)
+                    act_copy(later, d).wait_send()
+
+            make_act(later)
+            for d in range(1, n):
+                act_copy(later, d).start()
 
         return carry
 
@@ -266,11 +287,12 @@
         def _(q=q):
             pipe_copy(q).wait_send()
 
-    for slot in range(min(RING, steps)):
-        for d in range(1, n):
-            spread(act, a_send, a_recv, slot, d).wait_send()
-            spread(scaled, s_send, s_recv, slot, d).wait_send()
+    for d in range(1, n):
+        for slot in range(RING):
+            scaled_copy(slot, d).wait_send()
             part_copy(slot, d).wait_send()
+        for slot in range(min(HELD, steps)):
+            act_copy(slot, d).wait_send()
     for c in range(CHUNKS):
         @pl.when(has_prev)
         def _(c=c):
@@ -308,9 +330,10 @@
             pltpu.VMEM((hid, width), bf),
             pltpu.VMEM((ticks, CHUNKS, rows, width), bf),
             pltpu.VMEM((CHUNKS, rows, width), jnp.float32),
-            pltpu.VMEM((steps, rows, width), bf),
+            pltpu.VMEM((steps - CHUNKS, rows, width), bf),
+            pltpu.VMEM((HELD, n, rows, width), bf),
             pltpu.VMEM((RING, n, rows, width), bf),
-            pltpu.VMEM((RING, n, rows, width), bf),
+            pltpu.VMEM((CHUNKS, n * rows, hid), jnp.float32),
             pltpu.VMEM((n * rows, hid), bf),
             pltpu.VMEM((RING, n, rows, width), bf),
             pltpu.VMEM((RING, n - 1, rows, width), bf),
@@ -318,8 +341,8 @@
             pltpu.VMEM((steps, rows, width), bf),
             dma((2, tile_count)),
             dma((3,)),
-            dma((RING, n - 1)),
-            dma((RING, n - 1)),
+            dma((HELD, n - 1)),
+            dma((HELD, n - 1)),
             dma((RING, n - 1)),
             dma((RING, n - 1)),
             dma((RING, n - 1)),
@@ -330,7 +353,7 @@
             dma((CHUNKS,)),
         ],
         compiler_params=pltpu.CompilerParams(
-            collective_id=0, has_side_effects=True, vmem_limit_bytes=66 * 1024 * 1024 - 2 * 1024 * 1024
+            collective_id=0, has_side_effects=True, vmem_limit_bytes=67_043_328
         ),
     )(
         slot_order,
@@ -340,7 +363,7 @@
         down_w,
         stash.reshape(ticks, CHUNKS, rows, width),
         received.reshape(CHUNKS, rows, width),
-        landed.reshape(steps, rows, width),
+        landed[: ticks - 1].reshape(steps - CHUNKS, rows, width),
     )
     is_last = lax.axis_index("pipe") == sections - 1
     pending = jnp.where(is_last, landed[ticks - 1], pend.reshape(tokens, width)).astype(jnp.float32)

time: 267 us -> 220 us (0.82)
  Pallas kernels: 255 us -> 206 us
    pallas_call x1, Pallas kernels: 255 us -> 206 us  [shards(): pl.pallas_call(functools.partial(kernel, n, sections, steps), out_shape=(...]
where the time goes in v2:
time: 220 us; the launch traced here: 219 us
  Pallas kernels  206 us (94%)
  local copies, waits for them, and re-layouts  9.46 us (4%)
  other arithmetic  2.59 us (1%)
    pallas_call x1, Pallas kernels, shards(): pl.pallas_call(functools.partial(kernel, n, sections, steps), out_shape=(...  206 us

profile of v2, /device:TPU:1, one launch (start us, length us, event | category | flops | bytes accessed | tf_op | source)
XLA Modules:
  0.0 218.8 jit_solution(11663923519242007469)
XLA Ops:
  0.6 3.6 %copy.12 = bf16[3,4,8,2,2,3200]{5,4,2,3,1,0:T(2,128)(2,1)S(1)} copy(bf16[3,4,8,2,2,3200]{5,2,4,3,1,0:T(8,128)(2,1)} %bitcast.19) | data formatting | bytes 4915200 | tf_op jit(solution)/shard_map/reshape | solution.py:311
  4.2 0.6 slice.11
  4.8 1.1 slice.10
  5.9 1.5 reshape.50.landed_hbm
  7.5 1.2 squeeze.11
  8.7 206.1 %shard_map.95 = (bf16[6,64,3200]{2,1,0:T(8,128)(2,1)}, bf16[2,64,3200]{2,1,0:T(8,128)(2,1)}) custom-call(s32[1,3]{1,0:T(1,128)} %order.1, f32[1,3200]{1,0:T(1,128)} %gain.1, f32[1,3200]{1,0:T(1,128)} %lscale.1, bf16[3200,3200]{1,0:T(8,128)(2,1)} %bitcast.14, bf16[3200,3200]{1,0:T(8,128)(2,1)} %bitcast.15, bf16[3,2,64,3200]{3,2,1,0:T(8,128)(2,1)} %bitcast.18, ...), custom_call_target="tpu_custom_call" | custom-call | tf_op jit(solution)/shard_map/pallas_call | solution.py:320
  214.8 0.0 copy-start
  214.8 2.6 %fusion = f32[1,128,3200]{2,1,0:T(8,128)} fusion(bf16[1,128,3200]{2,1,0:T(8,128)(2,1)} %squeeze.11, pred[]{:T(512)S(6)} %eq.3, bf16[1,128,3200]{2,1,0:T(8,128)(2,1)} %bitcast.22), kind=kLoop, calls=%fused_computation.2 | loop fusion | flops 819200 | bytes 3276801 | tf_op jit(solution)/shard_map/convert_element_type | solution.py:369
  217.4 0.0 copy-done
  217.4 1.4 copy.14
Async XLA Ops:
  214.8 2.6 %copy-start = (bf16[6,64,3200]{2,1,0:T(8,128)(2,1)S(1)}, bf16[6,64,3200]{2,1,0:T(8,128)(2,1)}, u32[]{:S(2)}) copy-start(bf16[6,64,3200]{2,1,0:T(8,128)(2,1)} %get-tuple-element.4) | copy-start | bytes 7372804

commit v3 on v2

--- a/solution.py
+++ b/solution.py
@@ -10,7 +10,7 @@
 GRID = 16
 EPS = 1e-06
 CHUNKS = 2
-RING = 2
+RING = CHUNKS
 HELD = 2 * CHUNKS
 TILE = 512
 MESH = pl.DeviceIdType.MESH
@@ -175,11 +175,6 @@
         make_scaled(q)
         for d in range(1, n):
             scaled_copy(q, d).start()
-    ahead = min(CHUNKS + 1, steps)
-    for a in range(CHUNKS, ahead):
-        make_act(a)
-        for d in range(1, n):
-            act_copy(a, d).start()
     in_landed.wait()
 
     tokens = n * rows
@@ -188,91 +183,104 @@
         first = j * TILE
         return first if isinstance(j, int) else pl.multiple_of(first, TILE)
 
-    def step(q, carry):
-        slot, chunk = q % RING, q % CHUNKS
+    ticks = steps // CHUNKS
+
+    def send_act(a):
+        @pl.when(a >= HELD)
+        def _():
+            for d in range(1, n):
+                act_copy(a, d).wait_send()
+
+        make_act(a)
+        for d in range(1, n):
+            act_copy(a, d).start()
+
+    def send_next(q):
+        for d in range(1, n):
+            scaled_copy(q, d).wait_send()
+        next_grads(q)
+        make_scaled(q)
+        for d in range(1, n):
+            scaled_copy(q, d).start()
+
+    def tick_of(tick, carry):
+        head = tick * CHUNKS
+        more = tick + 1 < ticks
 
         def arrive(which, j, size):
-            @pl.when(q == 0)
+            @pl.when(tick == 0)
             def _():
                 weight_copies(j, size)[which].wait()
 
         def hidden_tile(j, size):
             arrive(0, j, size)
             span = pl.ds(aligned(j), size)
-            rows_of = act[pl.ds(q % HELD, CHUNKS)].reshape(CHUNKS * tokens, width)
+            rows_of = act[pl.ds(head % HELD, CHUNKS)].reshape(CHUNKS * tokens, width)
             hidden = lax.dot_general(rows_of, up_w[span, :], NT, preferred_element_type=jnp.float32)
             factor_of[:, :, span] = gelu_slope(hidden).reshape(CHUNKS, tokens, size)
 
-        @pl.when(chunk == 0)
-        def _():
-            for c in range(CHUNKS):
-                for d in range(1, n):
-                    act_copy(q + c, d).wait_recv()
-            pl.loop(0, full)(lambda j: hidden_tile(j, TILE))
+        for c in range(CHUNKS):
+            for d in range(1, n):
+                act_copy(head + c, d).wait_recv()
+        pl.loop(0, full)(lambda j: hidden_tile(j, TILE))
+        if rem:
+            hidden_tile(full, rem)
+
+        @pl.when(tick >= 1)
+        def _():
+            send_next(head + CHUNKS - 1)
+
+        @pl.when(more)
+        def _():
+            send_act(head + CHUNKS)
+
+        for c in range(CHUNKS):
+            q = head + c
+            for d in range(1, n):
+                scaled_copy(q, d).wait_recv()
+
+            def up_tile(j, size):
+                if c == 0:
+                    arrive(1, j, size)
+                span = pl.ds(aligned(j), size)
+                upstream = lax.dot_general(
+                    scaled[c].reshape(tokens, width), down_w[span, :], NT, preferred_element_type=jnp.float32
+                )
+                slope[:, span] = (upstream * factor_of[c, :, span]).astype(jnp.bfloat16)
+
+            pl.loop(0, full)(lambda j: up_tile(j, TILE))
             if rem:
-                hidden_tile(full, rem)
-
-        for d in range(1, n):
-            scaled_copy(q, d).wait_recv()
-
-        def up_tile(j, size):
-            arrive(1, j, size)
-            span = pl.ds(aligned(j), size)
-            upstream = lax.dot_general(
-                scaled[slot].reshape(tokens, width), down_w[span, :], NT, preferred_element_type=jnp.float32
-            )
-            slope[:, span] = (upstream * factor_of[chunk, :, span]).astype(jnp.bfloat16)
-
-        pl.loop(0, full)(lambda j: up_tile(j, TILE))
-        if rem:
-            up_tile(full, rem)
-
-        @pl.when(q >= 1)
-        def _():
-            finish(q - 1)
-
-        @pl.when(q >= RING)
-        def _():
-            for d in range(1, n):
-                part_copy(slot, d).wait_send()
-
-        def down_tile(j, size):
-            span = pl.ds(aligned(j), size)
-            part = jnp.dot(slope[...], up_w[:, span], preferred_element_type=jnp.float32)
-            psend[slot, :, :, span] = part.astype(jnp.bfloat16).reshape(n, rows, size)
-            for d in range(1, n):
-                part_copy(slot, d, span).start()
-
-        pl.loop(0, wfull)(lambda j: down_tile(j, TILE))
-        if wrem:
-            down_tile(wfull, wrem)
-
-        @pl.when((q + 1 >= CHUNKS) & (q + 1 < steps))
-        def _():
-            for d in range(1, n):
-                scaled_copy(q + 1, d).wait_send()
-            next_grads(q + 1)
-            make_scaled(q + 1)
-            for d in range(1, n):
-                scaled_copy(q + 1, d).start()
-
-        @pl.when(q + ahead < steps)
-        def _():
-            later = q + ahead
-
-            @pl.when(later >= HELD)
+                up_tile(full, rem)
+            if c:
+                finish(q - 1)
+
+            @pl.when(tick >= 1)
             def _():
                 for d in range(1, n):
-                    act_copy(later, d).wait_send()
-
-            make_act(later)
-            for d in range(1, n):
-                act_copy(later, d).start()
-
+                    part_copy(c, d).wait_send()
+
+            def down_tile(j, size):
+                span = pl.ds(aligned(j), size)
+                part = jnp.dot(slope[...], up_w[:, span], preferred_element_type=jnp.float32)
+                psend[c, :, :, span] = part.astype(jnp.bfloat16).reshape(n, rows, size)
+                for d in range(1, n):
+                    part_copy(c, d, span).start()
+
+            pl.loop(0, wfull)(lambda j: down_tile(j, TILE))
+            if wrem:
+                down_tile(wfull, wrem)
+
+            @pl.when(more)
+            def _():
+                if c:
+                    send_next(q - 1 + CHUNKS)
+                if c + 1 < CHUNKS:
+                    send_act(q + 1 + CHUNKS)
+
+        finish(head + CHUNKS - 1)
         return carry
 
-    lax.fori_loop(0, steps, step, 0)
-    finish(steps - 1)
+    lax.fori_loop(0, ticks, tick_of, 0)
 
     for q in range(steps - CHUNKS, steps):
         @pl.when(has_prev)

time: 220 us -> 204 us (0.927)
  Pallas kernels: 206 us -> 191 us
    pallas_call x1, Pallas kernels: 206 us -> 191 us  [shards(): pl.pallas_call(functools.partial(kernel, n, sections, steps), out_shape=(...]
where the time goes in v3:
time: 204 us
  Pallas kernels  191 us (94%)
  local copies, waits for them, and re-layouts  9.46 us (5%)
  other arithmetic  2.59 us (1%)
    pallas_call x1, Pallas kernels, shards(): pl.pallas_call(functools.partial(kernel, n, sections, steps), out_shape=(...  191 us

profile of v3, /device:TPU:1, one launch (start us, length us, event | category | flops | bytes accessed | tf_op | source)
XLA Modules:
  0.0 203.7 jit_solution(11925681515953142390)
XLA Ops:
  0.6 3.6 %copy.12 = bf16[3,4,8,2,2,3200]{5,4,2,3,1,0:T(2,128)(2,1)S(1)} copy(bf16[3,4,8,2,2,3200]{5,2,4,3,1,0:T(8,128)(2,1)} %bitcast.19) | data formatting | bytes 4915200 | tf_op jit(solution)/shard_map/reshape | solution.py:319
  4.2 0.6 slice.11
  4.8 1.1 slice.10
  5.9 1.5 reshape.50.landed_hbm
  7.5 1.2 squeeze.11
  8.7 191.0 %shard_map.95 = (bf16[6,64,3200]{2,1,0:T(8,128)(2,1)}, bf16[2,64,3200]{2,1,0:T(8,128)(2,1)}) custom-call(s32[1,3]{1,0:T(1,128)} %order.1, f32[1,3200]{1,0:T(1,128)} %gain.1, f32[1,3200]{1,0:T(1,128)} %lscale.1, bf16[3200,3200]{1,0:T(8,128)(2,1)} %bitcast.14, bf16[3200,3200]{1,0:T(8,128)(2,1)} %bitcast.15, bf16[3,2,64,3200]{3,2,1,0:T(8,128)(2,1)} %bitcast.18, ...), custom_call_target="tpu_custom_call" | custom-call | tf_op jit(solution)/shard_map/pallas_call | solution.py:328
  199.7 0.0 copy-start
  199.7 2.6 %fusion = f32[1,128,3200]{2,1,0:T(8,128)} fusion(bf16[1,128,3200]{2,1,0:T(8,128)(2,1)} %squeeze.11, pred[]{:T(512)S(6)} %eq.3, bf16[1,128,3200]{2,1,0:T(8,128)(2,1)} %bitcast.22), kind=kLoop, calls=%fused_computation.2 | loop fusion | flops 819200 | bytes 3276801 | tf_op jit(solution)/shard_map/convert_element_type | solution.py:377
  202.3 0.0 copy-done
  202.3 1.4 copy.14
Async XLA Ops:
  199.7 2.6 %copy-start = (bf16[6,64,3200]{2,1,0:T(8,128)(2,1)S(1)}, bf16[6,64,3200]{2,1,0:T(8,128)(2,1)}, u32[]{:S(2)}) copy-start(bf16[6,64,3200]{2,1,0:T(8,128)(2,1)} %get-tuple-element.4) | copy-start | bytes 7372804
